TPU v7x, 128 devices: a whole 4x4x4 slice. The times are simulated.
128 devices in a mesh: req: 32 (over z, y, core), tok: 4 (over x).
Axes of the slice: x: 4, y: 4, z: 4, core: 2. Of those that a mesh axis runs over, the one named last changes fastest.
Arguments:
- tokens: bfloat16 [32768, 2048], P(('req', 'tok')), may hold values from -12 to 12
- attention_norm_gain: float32 [2048], replicated, may hold values from 0.1 to 1.9
- attention_norm_bias: float32 [2048], replicated, may hold values from -1.75 to 1.75
- query_key_value_matrix: bfloat16 [3, 2048, 2048], P(None, 'req', 'tok'), may hold values from -0.125 to 0.125
- query_key_value_bias: float32 [3, 2048], P(None, 'tok'), may hold values from -3 to 3
- output_matrix: bfloat16 [4, 512, 2048], P('tok', 'req'), may hold values from -0.125 to 0.125
- feedforward_norm_gain: float32 [2048], replicated, may hold values from 0.1 to 1.9
- feedforward_norm_bias: float32 [2048], replicated, may hold values from -1.75 to 1.75
- gate_up_matrix: bfloat16 [2, 2048, 2816], P(None, 'req', 'tok'), may hold values from -0.125 to 0.125
- down_matrix: bfloat16 [4, 704, 2048], P('tok', 'req'), may hold values from -0.109375 to 0.109375
- adapter_input_query_key_value: bfloat16 [64, 48, 2048], P(None, None, 'req'), may hold values from -0.125 to 0.125
- adapter_output_query_key_value: bfloat16 [64, 48, 4, 512], P(None, None, 'tok', 'req'), may hold values from -0.75 to 0.75
- adapter_input_output: bfloat16 [64, 16, 4, 512], P(None, None, 'tok', 'req'), may hold values from -0.125 to 0.125
- adapter_output_projection: bfloat16 [64, 16, 2048], P(None, None, 'req'), may hold values from -0.75 to 0.75
- adapter_input_gate_up: bfloat16 [64, 32, 2048], P(None, None, 'req'), may hold values from -0.125 to 0.125
- adapter_output_gate_up: bfloat16 [64, 32, 4, 704], P(None, None, 'tok', 'req'), may hold values from -0.75 to 0.75
- adapter_input_down: bfloat16 [64, 16, 4, 704], P(None, None, 'tok', 'req'), may hold values from -0.109375 to 0.109375
- adapter_output_down: bfloat16 [64, 16, 2048], P(None, None, 'req'), may hold values from -0.75 to 0.75
- lengths: int32 [32, 4], P('req'), may hold values from 1 to 511, 1024 in all within a row
- adapter_per_request: int32 [32, 4], replicated, may hold values from 0 to 63
Outputs:
- layer_out: bfloat16 [32768, 2048], P(('req', 'tok'))
Inputs may be any that keep to these rules, and one draw needn't show every extreme that they name: Each row holds one owner's 4 prompt lengths in order; they sum to 1024, and the longest is 511 in every row.
All inputs are finite; a program needn't handle non-finite values.
Results may differ from a plain program's by a relative error of at most 0.02.
Values may be sent and summed in bfloat16 or wider, within the bound.
A program may use at most 128 MiB of HBM per device.

v0:
```python
import math

import jax
import jax.numpy as jnp
from jax import lax
from jax.sharding import PartitionSpec as P

HD = 64
ROT = 16


def layer_norm(values, gain_vec, shift_bias):
    row_mean = jnp.mean(values, axis=-1, keepdims=True)
    centered = values - row_mean
    variance = jnp.mean(centered * centered, axis=-1, keepdims=True)
    return centered * lax.rsqrt(variance + 1e-05) * gain_vec + shift_bias


def rotate(values, positions):
    half_rot = ROT // 2
    frequency = jnp.exp(-math.log(10000.0) * (2.0 * jnp.arange(half_rot, dtype=jnp.float32) / ROT))
    angles = positions.astype(jnp.float32)[:, None] * frequency[None, :]
    cosine = jnp.cos(angles)[:, None, :]
    sine_part = jnp.sin(angles)[:, None, :]
    lower_half = values[..., :half_rot]
    upper_half = values[..., half_rot:ROT]
    return jnp.concatenate(
        [
            lower_half * cosine - upper_half * sine_part,
            upper_half * cosine + lower_half * sine_part,
            values[..., ROT:],
        ],
        axis=-1,
    )


def request_layout(owner_lengths, row_count):
    request_end = jnp.cumsum(owner_lengths)
    request_begin = request_end - owner_lengths
    places = jnp.arange(row_count, dtype=jnp.int32)
    request_slot = jnp.sum((places[:, None] >= request_end[None, :]).astype(jnp.int32), axis=1)
    member_mask = (
        request_slot[:, None] == jnp.arange(owner_lengths.shape[0], dtype=jnp.int32)[None, :]
    )
    request_start = jnp.sum(jnp.where(member_mask, request_begin[None, :], 0), axis=1)
    return (places, request_slot, member_mask, request_start)


def contract_rows(operand, weight):
    return jnp.einsum(
        "tn,knc->tkc",
        operand,
        lax.all_gather(weight, "req", axis=1, tiled=True),
        preferred_element_type=jnp.float32,
    )


def gather_rows(local_rows):
    return lax.all_gather(local_rows, "tok", axis=0, tiled=True)


def reduce_rows(partial_value):
    return lax.psum_scatter(
        partial_value.astype(jnp.bfloat16), "tok", scatter_dimension=0, tiled=True
    ).astype(jnp.float32)


def low_rank(operand, shrink, member_weight):
    all_ranks = jnp.einsum("tn,jkn->tjk", operand, shrink, preferred_element_type=jnp.float32)
    chosen = lax.optimization_barrier(
        jnp.sum(member_weight[:, :, None] * all_ranks, axis=1).astype(jnp.bfloat16)
    )
    return member_weight[:, :, None].astype(jnp.bfloat16) * chosen[:, None, :]


def flatten_last(divide_portion):
    return divide_portion.reshape(divide_portion.shape[0], divide_portion.shape[1], -1)


def attention(query, key_rows, value_rows, request_slot, places):
    row_count, head_count, head_size = query.shape
    block_rows = min(512, row_count)
    block_count = row_count // block_rows
    score_scale = head_size ** (-0.5)

    def query_block(query_idx, attended_all):
        query_start = query_idx * block_rows
        query_part = lax.dynamic_slice_in_dim(query, query_start, block_rows, 0)
        query_slot = lax.dynamic_slice_in_dim(request_slot, query_start, block_rows, 0)
        query_place = lax.dynamic_slice_in_dim(places, query_start, block_rows, 0)

        def key_block(key_idx, state_pair):
            numerator, denominator = state_pair
            key_start = key_idx * block_rows
            key_part = lax.dynamic_slice_in_dim(key_rows, key_start, block_rows, 0)
            value_part = lax.dynamic_slice_in_dim(value_rows, key_start, block_rows, 0)
            key_slot = lax.dynamic_slice_in_dim(request_slot, key_start, block_rows, 0)
            key_place = lax.dynamic_slice_in_dim(places, key_start, block_rows, 0)
            scores = (
                jnp.einsum("qhd,khd->hqk", query_part, key_part, preferred_element_type=jnp.float32)
                * score_scale
            )
            visible = (query_slot[:, None] == key_slot[None, :]) & (
                key_place[None, :] <= query_place[:, None]
            )
            weights = jnp.where(visible[None], jnp.exp(scores), 0.0)
            numerator = numerator + jnp.einsum(
                "hqk,khd->qhd",
                weights.astype(jnp.bfloat16),
                value_part,
                preferred_element_type=jnp.float32,
            )
            denominator = denominator + jnp.sum(weights, axis=2)
            return (numerator, denominator)

        start_pair = (
            jnp.zeros((block_rows, head_count, head_size), jnp.float32),
            jnp.zeros((head_count, block_rows), jnp.float32),
        )
        numerator, denominator = lax.fori_loop(0, block_count, key_block, start_pair)
        block_out = (numerator / jnp.transpose(denominator)[:, :, None]).astype(jnp.bfloat16)
        return lax.dynamic_update_slice_in_dim(attended_all, block_out, query_start, 0)

    return lax.fori_loop(0, block_count, query_block, jnp.zeros_like(query))


def on_device(
    tokens,
    attention_norm_gain,
    attention_norm_bias,
    query_key_value_matrix,
    query_key_value_bias,
    output_matrix,
    feedforward_norm_gain,
    feedforward_norm_bias,
    gate_up_matrix,
    down_matrix,
    adapter_input_query_key_value,
    adapter_output_query_key_value,
    adapter_input_output,
    adapter_output_projection,
    adapter_input_gate_up,
    adapter_output_gate_up,
    adapter_input_down,
    adapter_output_down,
    lengths,
    adapter_per_request,
):
    tok_count = lax.axis_size("tok")
    scatter_portions = [
        adapter_input_query_key_value,
        adapter_output_projection,
        adapter_input_gate_up,
        adapter_output_down,
    ]
    narrow_parts = [
        flatten_last(divide_portion)
        for divide_portion in (
            adapter_output_query_key_value,
            adapter_input_output,
            adapter_output_gate_up,
            adapter_input_down,
        )
    ]
    picked = [
        divide_portion[adapter_per_request] for divide_portion in scatter_portions + narrow_parts
    ]
    fetched = (
        lax.all_to_all(picked[0], "req", split_axis=0, concat_axis=3, tiled=True),
        lax.all_to_all(picked[1], "req", split_axis=0, concat_axis=3, tiled=True),
        lax.all_to_all(picked[2], "req", split_axis=0, concat_axis=3, tiled=True),
        lax.all_to_all(picked[3], "req", split_axis=0, concat_axis=3, tiled=True),
        lax.all_to_all(picked[4], "req", split_axis=0, concat_axis=3, tiled=True),
        lax.all_to_all(picked[5], "req", split_axis=0, concat_axis=3, tiled=True),
        lax.all_to_all(picked[6], "req", split_axis=0, concat_axis=3, tiled=True),
        lax.all_to_all(picked[7], "req", split_axis=0, concat_axis=3, tiled=True),
    )
    (
        narrow_query_key_value,
        widen_output,
        narrow_gate,
        widen_down,
        widen_query_key_value,
        narrow_output,
        widen_gate,
        narrow_down,
    ) = [arrived[0] for arrived in fetched]
    row_count = tokens.shape[0] * tok_count
    places, request_slot, member_mask, request_start = request_layout(lengths[0], row_count)
    member_weight = member_mask.astype(jnp.float32)
    positions = places - request_start
    rank_size = narrow_output.shape[1]
    slot_count = narrow_output.shape[0]
    normed = layer_norm(
        tokens.astype(jnp.float32), attention_norm_gain, attention_norm_bias
    ).astype(jnp.bfloat16)
    gathered = gather_rows(normed)
    head_cols = query_key_value_matrix.shape[2]
    low_qkv = low_rank(gathered, narrow_query_key_value, member_weight).reshape(
        row_count, slot_count, 3, rank_size
    )
    mixed = contract_rows(gathered, query_key_value_matrix) + query_key_value_bias[None]
    mixed = mixed + jnp.einsum(
        "tjkr,jkrc->tkc",
        low_qkv,
        widen_query_key_value.reshape(slot_count, 3, rank_size, head_cols),
        preferred_element_type=jnp.float32,
    )
    head_count = head_cols // HD
    query = rotate(mixed[:, 0].reshape(row_count, head_count, HD), positions).astype(jnp.bfloat16)
    key_rows = rotate(mixed[:, 1].reshape(row_count, head_count, HD), positions).astype(
        jnp.bfloat16
    )
    value_rows = mixed[:, 2].reshape(row_count, head_count, HD).astype(jnp.bfloat16)
    attended = attention(query, key_rows, value_rows, request_slot, places).reshape(
        row_count, head_cols
    )
    out_term = contract_rows(attended, output_matrix)[:, 0]
    out_term = out_term + jnp.einsum(
        "tjr,jrd->td",
        low_rank(attended, narrow_output, member_weight),
        widen_output,
        preferred_element_type=jnp.float32,
    )
    residual = (tokens.astype(jnp.float32) + reduce_rows(out_term)).astype(jnp.bfloat16)
    normed2 = layer_norm(
        residual.astype(jnp.float32), feedforward_norm_gain, feedforward_norm_bias
    ).astype(jnp.bfloat16)
    gathered2 = gather_rows(normed2)
    hidden_cols = gate_up_matrix.shape[2]
    low_gate = low_rank(gathered2, narrow_gate, member_weight).reshape(
        row_count, slot_count, 2, rank_size
    )
    gate_up = contract_rows(gathered2, gate_up_matrix)
    gate_up = gate_up + jnp.einsum(
        "tjkr,jkrf->tkf",
        low_gate,
        widen_gate.reshape(slot_count, 2, rank_size, hidden_cols),
        preferred_element_type=jnp.float32,
    )
    hidden = (jax.nn.silu(gate_up[:, 0]) * gate_up[:, 1]).astype(jnp.bfloat16)
    down_term = contract_rows(hidden, down_matrix)[:, 0]
    down_term = down_term + jnp.einsum(
        "tjr,jrd->td",
        low_rank(hidden, narrow_down, member_weight),
        widen_down,
        preferred_element_type=jnp.float32,
    )
    return (residual.astype(jnp.float32) + reduce_rows(down_term)).astype(jnp.bfloat16)


def solution(mesh):
    in_specs = (
        P(("req", "tok"), None),
        P(),
        P(),
        P(None, "req", "tok"),
        P(None, "tok"),
        P("tok", "req", None),
        P(),
        P(),
        P(None, "req", "tok"),
        P("tok", "req", None),
        P(None, None, "req"),
        P(None, None, "tok", "req"),
        P(None, None, "tok", "req"),
        P(None, None, "req"),
        P(None, None, "req"),
        P(None, None, "tok", "req"),
        P(None, None, "tok", "req"),
        P(None, None, "req"),
        P("req", None),
        P(),
    )
    out_specs = P(("req", "tok"), None)
    return jax.shard_map(
        on_device, mesh=mesh, in_specs=in_specs, out_specs=out_specs, check_vma=False
    )
```

profile of v0, /device:TPU:1, one launch (start us, length us, event | category | flops | bytes accessed | tf_op | source)
XLA Modules:
  0.0 455.8 jit_solution(17531012510787143628)
XLA Ops:
  15.7 9.6 %all-to-all-start.2 = ((bf16[32,2,512]{2,1,0:T(2,128)(2,1)}), bf16[32,2,512]{2,1,0:T(2,128)(2,1)S(1)}, u32[]{:S(2)}, u32[]{:S(2)}) async-start(bf16[32,2,512]{2,1,0:T(2,128)(2,1)} %reshape.344), calls=%async_computation.2 | async-start | bytes 131072 | tf_op jit(solution)/shard_map/all_to_all | solution.py:174
  32.6 5.5 %all-to-all-start = ((bf16[32,2,1536]{2,1,0:T(2,128)(2,1)}), bf16[32,2,1536]{2,1,0:T(2,128)(2,1)S(1)}, u32[]{:S(2)}, u32[]{:S(2)}) async-start(bf16[32,2,1536]{2,1,0:T(2,128)(2,1)} %reshape.338), calls=%async_computation | async-start | bytes 393216 | tf_op jit(solution)/shard_map/all_to_all | solution.py:173
  38.1 8.2 %all-to-all-done = bf16[32,2,1536]{2,1,0:T(2,128)(2,1)S(1)} async-done(((bf16[32,2,1536]{2,1,0:T(2,128)(2,1)}), bf16[32,2,1536]{2,1,0:T(2,128)(2,1)S(1)}, u32[]{:S(2)}, u32[]{:S(2)}) %all-to-all-start) | async-done | bytes 196640 | tf_op jit(solution)/shard_map/all_to_all | solution.py:173
  46.3 3.8 all-to-all-start.3
  53.0 6.0 %all-to-all-done.3 = bf16[32,2,2048]{2,1,0:T(2,128)(2,1)S(1)} async-done(((bf16[32,2,2048]{2,1,0:T(2,128)(2,1)}), bf16[32,2,2048]{2,1,0:T(2,128)(2,1)S(1)}, u32[]{:S(2)}, u32[]{:S(2)}) %all-to-all-start.3) | async-done | bytes 262176 | tf_op jit(solution)/shard_map/all_to_all | solution.py:170
  73.0 4.1 all-to-all-done.1
  86.8 29.5 %all-gather.9.cloned.1.call-done = bf16[3,2048,512]{2,1,0:T(8,128)(2,1)} async-done(((bf16[3,64,512]{2,1,0:T(8,128)(2,1)}), bf16[3,2048,512]{2,1,0:T(8,128)(2,1)}) %all-gather.9.cloned.1.call-update) | async-done | bytes 6291472 | tf_op jit(solution)/shard_map/all_gather | solution.py:53
  116.3 10.3 %fusion.29 = f32[1024,3,512]{0,2,1:T(8,128)S(1)} fusion(bf16[3,2048,512]{2,1,0:T(8,128)(2,1)} %all-gather.9.cloned.1.call-done, bf16[1024,2048]{1,0:T(8,128)(2,1)} %all-gather.7.cloned.1.call-done), kind=kOutput, calls=%fused_computation.41 | convolution fusion | flops 6442450944 | bytes 16777216 | tf_op jit(solution)/shard_map/tn,knc->tkc/dot_general | solution.py:50
  131.5 52.5 %while.48 = (s32[]{:T(128)}, bf16[1024,8,64]{0,2,1:T(8,128)(2,1)}, bf16[1024,8,64]{0,2,1:T(8,128)(2,1)}, s32[1024]{0:T(1024)S(1)}, s32[1024]{0:T(1024)S(1)}, /*i...) while((s32[]{:T(128)}, bf16[1024,8,64]{0,2,1:T(8,128)(2,1)}, ...), condition=%wide.region_10.11_spmd.clone, body=%wide.region_6.10_spmd.clone.sunk | while | flops 551292928 | bytes 23962128 | solution.py:124
  132.8 24.1 %while.49 = (s32[]{:T(128)}, f32[512,8,64]{0,2,1:T(8,128)S(1)}, f32[8,512]{1,0:T(8,128)S(1)}, bf16[1024,8,64]{0,2,1:T(8,128)(2,1)S(1)}, s32[512]{0:T(512)S(1)}, ...) while((s32[]{:T(128)}, f32[512,8,64]{0,2,1:T(8,128)S(1)}, ...), condition=%wide.region_9.9_spmd.clone, body=%wide.region_7.8_spmd.clone.sunk | while | flops 550768640 | bytes 21315788 | solution.py:120
  133.3 6.4 %fusion.113 = (f32[8,512]{1,0:T(8,128)S(1)}, f32[8,512,512]{2,1,0:T(8,128)}) fusion(pred[512,512]{0,1:T(8,128)(4,1)S(1)} %compare_and_fusion.2, bf16[512,8,64]{0,2,1:T(8,128)(2,1)S(1)} %get-tuple-element.602, bf16[1024,8,64]{0,2,1:T(8,128)(2,1)} %get-tuple-element.601, s32[]{:T(128)S(6)} %select_n.66), kind=kOutput, calls=%fused_computation.9.clone.1 | convolution fusion | flops 274722816 | bytes 9715716 | tf_op jit(solution)/shard_map/while/body/eval_jaxpr/while/body/eval_jaxpr/qhd,khd->hqk/dot_general | solution.py:100
  139.7 5.1 %fusion.114 = f32[512,8,64]{0,2,1:T(8,128)S(1)} fusion(f32[8,512,512]{2,1,0:T(8,128)} %get-tuple-element.563, pred[512,512]{0,1:T(8,128)(4,1)S(1)} %compare_and_fusion.2, f32[512,8,64]{0,2,1:T(8,128)S(1)} %get-tuple-element.580, bf16[1024,8,64]{0,2,1:T(8,128)(2,1)S(1)} %get-tuple-element.596, s32[]{:T(128)S(6)} %select_n.66, pred[]{:T(512)S(6)} %compare.3), kind=kOutput, calls=%fused_computation.16.clone.1 | convolution fusion | flops 275251200 | bytes 11272197 | tf_op jit(solution)/shard_map/while/body/eval_jaxpr/while/body/eval_jaxpr/hqk,khd->qhd/dot_general | solution.py:107
  145.3 6.4 %fusion.113 = (f32[8,512]{1,0:T(8,128)S(1)}, f32[8,512,512]{2,1,0:T(8,128)}) fusion(pred[512,512]{0,1:T(8,128)(4,1)S(1)} %compare_and_fusion.2, bf16[512,8,64]{0,2,1:T(8,128)(2,1)S(1)} %get-tuple-element.602, bf16[1024,8,64]{0,2,1:T(8,128)(2,1)} %get-tuple-element.601, s32[]{:T(128)S(6)} %select_n.66), kind=kOutput, calls=%fused_computation.9.clone.1 | convolution fusion | flops 274722816 | bytes 9715716 | tf_op jit(solution)/shard_map/while/body/eval_jaxpr/while/body/eval_jaxpr/qhd,khd->hqk/dot_general | solution.py:100
  151.7 5.1 %fusion.114 = f32[512,8,64]{0,2,1:T(8,128)S(1)} fusion(f32[8,512,512]{2,1,0:T(8,128)} %get-tuple-element.563, pred[512,512]{0,1:T(8,128)(4,1)S(1)} %compare_and_fusion.2, f32[512,8,64]{0,2,1:T(8,128)S(1)} %get-tuple-element.580, bf16[1024,8,64]{0,2,1:T(8,128)(2,1)S(1)} %get-tuple-element.596, s32[]{:T(128)S(6)} %select_n.66, pred[]{:T(512)S(6)} %compare.3), kind=kOutput, calls=%fused_computation.16.clone.1 | convolution fusion | flops 275251200 | bytes 11272197 | tf_op jit(solution)/shard_map/while/body/eval_jaxpr/while/body/eval_jaxpr/hqk,khd->qhd/dot_general | solution.py:107
  159.1 24.0 %while.49 = (s32[]{:T(128)}, f32[512,8,64]{0,2,1:T(8,128)S(1)}, f32[8,512]{1,0:T(8,128)S(1)}, bf16[1024,8,64]{0,2,1:T(8,128)(2,1)S(1)}, s32[512]{0:T(512)S(1)}, ...) while((s32[]{:T(128)}, f32[512,8,64]{0,2,1:T(8,128)S(1)}, ...), condition=%wide.region_9.9_spmd.clone, body=%wide.region_7.8_spmd.clone.sunk | while | flops 550768640 | bytes 21315788 | solution.py:120
  159.5 6.4 %fusion.113 = (f32[8,512]{1,0:T(8,128)S(1)}, f32[8,512,512]{2,1,0:T(8,128)}) fusion(pred[512,512]{0,1:T(8,128)(4,1)S(1)} %compare_and_fusion.2, bf16[512,8,64]{0,2,1:T(8,128)(2,1)S(1)} %get-tuple-element.602, bf16[1024,8,64]{0,2,1:T(8,128)(2,1)} %get-tuple-element.601, s32[]{:T(128)S(6)} %select_n.66), kind=kOutput, calls=%fused_computation.9.clone.1 | convolution fusion | flops 274722816 | bytes 9715716 | tf_op jit(solution)/shard_map/while/body/eval_jaxpr/while/body/eval_jaxpr/qhd,khd->hqk/dot_general | solution.py:100
  165.9 5.1 %fusion.114 = f32[512,8,64]{0,2,1:T(8,128)S(1)} fusion(f32[8,512,512]{2,1,0:T(8,128)} %get-tuple-element.563, pred[512,512]{0,1:T(8,128)(4,1)S(1)} %compare_and_fusion.2, f32[512,8,64]{0,2,1:T(8,128)S(1)} %get-tuple-element.580, bf16[1024,8,64]{0,2,1:T(8,128)(2,1)S(1)} %get-tuple-element.596, s32[]{:T(128)S(6)} %select_n.66, pred[]{:T(512)S(6)} %compare.3), kind=kOutput, calls=%fused_computation.16.clone.1 | convolution fusion | flops 275251200 | bytes 11272197 | tf_op jit(solution)/shard_map/while/body/eval_jaxpr/while/body/eval_jaxpr/hqk,khd->qhd/dot_general | solution.py:107
  171.5 6.4 %fusion.113 = (f32[8,512]{1,0:T(8,128)S(1)}, f32[8,512,512]{2,1,0:T(8,128)}) fusion(pred[512,512]{0,1:T(8,128)(4,1)S(1)} %compare_and_fusion.2, bf16[512,8,64]{0,2,1:T(8,128)(2,1)S(1)} %get-tuple-element.602, bf16[1024,8,64]{0,2,1:T(8,128)(2,1)} %get-tuple-element.601, s32[]{:T(128)S(6)} %select_n.66), kind=kOutput, calls=%fused_computation.9.clone.1 | convolution fusion | flops 274722816 | bytes 9715716 | tf_op jit(solution)/shard_map/while/body/eval_jaxpr/while/body/eval_jaxpr/qhd,khd->hqk/dot_general | solution.py:100
  178.0 5.1 %fusion.114 = f32[512,8,64]{0,2,1:T(8,128)S(1)} fusion(f32[8,512,512]{2,1,0:T(8,128)} %get-tuple-element.563, pred[512,512]{0,1:T(8,128)(4,1)S(1)} %compare_and_fusion.2, f32[512,8,64]{0,2,1:T(8,128)S(1)} %get-tuple-element.580, bf16[1024,8,64]{0,2,1:T(8,128)(2,1)S(1)} %get-tuple-element.596, s32[]{:T(128)S(6)} %select_n.66, pred[]{:T(512)S(6)} %compare.3), kind=kOutput, calls=%fused_computation.16.clone.1 | convolution fusion | flops 275251200 | bytes 11272197 | tf_op jit(solution)/shard_map/while/body/eval_jaxpr/while/body/eval_jaxpr/hqk,khd->qhd/dot_general | solution.py:107
  185.7 4.0 fusion.49
  193.1 45.2 %reduce-scatter.3.cloned.1.call-done = bf16[256,2048]{1,0:T(8,128)(2,1)} async-done(((bf16[1024,2048]{1,0:T(8,128)(2,1)}), bf16[256,2048]{1,0:T(8,128)(2,1)}) %reduce-scatter.3.cloned.1.call-update) | async-done | bytes 1048592 | tf_op jit(solution)/shard_map/reduce_scatter | solution.py:63
  246.4 7.9 %all-to-all-start.6 = ((bf16[32,2,704]{2,1,0:T(2,128)(2,1)}), bf16[32,2,704]{2,1,0:T(2,128)(2,1)S(1)}, u32[]{:S(2)}, u32[]{:S(2)}) async-start(bf16[32,2,704]{2,1,0:T(2,128)(2,1)} %reshape.352), calls=%async_computation.7 | async-start | bytes 196608 | tf_op jit(solution)/shard_map/all_to_all | solution.py:176
  257.0 4.7 %all-to-all-done.6 = bf16[32,2,704]{2,1,0:T(2,128)(2,1)S(1)} async-done(((bf16[32,2,704]{2,1,0:T(2,128)(2,1)}), bf16[32,2,704]{2,1,0:T(2,128)(2,1)S(1)}, u32[]{:S(2)}, u32[]{:S(2)}) %all-to-all-start.6) | async-done | bytes 90144 | tf_op jit(solution)/shard_map/all_to_all | solution.py:176
  261.7 3.9 all-to-all-start.4
  267.5 6.4 %all-to-all-done.4 = bf16[32,2,1408]{2,1,0:T(2,128)(2,1)S(1)} async-done(((bf16[32,2,1408]{2,1,0:T(2,128)(2,1)}), bf16[32,2,1408]{2,1,0:T(2,128)(2,1)S(1)}, u32[]{:S(2)}, u32[]{:S(2)}) %all-to-all-start.4) | async-done | bytes 180256 | tf_op jit(solution)/shard_map/all_to_all | solution.py:175
  273.8 3.8 all-to-all-start.7
  280.0 6.6 %all-to-all-done.7 = bf16[32,2,2048]{2,1,0:T(2,128)(2,1)S(1)} async-done(((bf16[32,2,2048]{2,1,0:T(2,128)(2,1)}), bf16[32,2,2048]{2,1,0:T(2,128)(2,1)S(1)}, u32[]{:S(2)}, u32[]{:S(2)}) %all-to-all-start.7) | async-done | bytes 262176 | tf_op jit(solution)/shard_map/all_to_all | solution.py:172
  310.0 32.2 %all-gather.15.cloned.1.call-done = bf16[2,2048,704]{2,1,0:T(8,128)(2,1)} async-done(((bf16[2,64,704]{2,1,0:T(8,128)(2,1)}), bf16[2,2048,704]{2,1,0:T(8,128)(2,1)}) %all-gather.15.cloned.1.call-update) | async-done | bytes 5767184 | tf_op jit(solution)/shard_map/all_gather | solution.py:53
  342.2 9.6 %fusion.25 = f32[1024,2,704]{0,2,1:T(8,128)S(1)} fusion(bf16[2,2048,704]{2,1,0:T(8,128)(2,1)} %all-gather.15.cloned.1.call-done, bf16[1024,2048]{1,0:T(8,128)(2,1)} %all-gather.13.cloned.1.call-done), kind=kOutput, calls=%fused_computation.37 | convolution fusion | flops 5905580032 | bytes 15728640 | tf_op jit(solution)/shard_map/tn,knc->tkc/dot_general | solution.py:50
  354.0 37.4 %all-gather.17.cloned.1.call-done = bf16[1,704,2048]{2,0,1:T(2,128)(2,1)} async-done(((bf16[1,22,2048]{2,0,1:T(2,128)(2,1)}), bf16[1,704,2048]{2,0,1:T(2,128)(2,1)}) %all-gather.17.cloned.1.call-update) | async-done | bytes 2883600 | tf_op jit(solution)/shard_map/all_gather | solution.py:53
  391.4 6.1 %fusion.32 = f32[1024,2048]{1,0:T(8,128)S(1)} fusion(bf16[1,704,2048]{2,0,1:T(2,128)(2,1)} %all-gather.17.cloned.1.call-done, bf16[1024,1,704]{0,2,1:T(8,128)(2,1)S(1)} %fusion.31), kind=kOutput, calls=%fused_computation.51 | convolution fusion | flops 2952790016 | bytes 12713984 | tf_op jit(solution)/shard_map/tn,knc->tkc/dot_general | solution.py:50
  400.7 45.5 %reduce-scatter.5.cloned.1.call-done = bf16[256,2048]{1,0:T(8,128)(2,1)} async-done(((bf16[1024,2048]{1,0:T(8,128)(2,1)}), bf16[256,2048]{1,0:T(8,128)(2,1)}) %reduce-scatter.5.cloned.1.call-update) | async-done | bytes 1048592 | tf_op jit(solution)/shard_map/reduce_scatter | solution.py:63
  (193 shorter events, 104.7 us)
Async XLA Ops:
  6.5 43.7 %copy-start = (bf16[64,48,64]{2,1,0:T(8,128)(2,1)S(1)}, bf16[64,48,64]{2,1,0:T(8,128)(2,1)}, u32[]{:S(2)}) copy-start(bf16[64,48,64]{2,1,0:T(8,128)(2,1)} %param.34) | copy-start | bytes 1179652
  6.5 76.5 %all-gather.7.cloned.1.call-start = ((), (), s32[]{:S(2)}) async-start(), calls=%async_computation.10 | async-start | bytes 5242880 | tf_op jit(solution)/shard_map/all_gather | solution.py:59
  9.7 16.3 %copy-start.12 = (bf16[64,48,1,16]{0,3,2,1:T(8,128)(2,1)S(1)}, bf16[64,48,1,16]{0,3,2,1:T(8,128)(2,1)}, u32[]{:S(2)}) copy-start(bf16[64,48,1,16]{0,3,2,1:T(8,128)(2,1)} %param.35) | copy-start | bytes 294916
  12.5 103.8 %all-gather.9.cloned.1.call-start = ((), (), s32[]{:S(2)}) async-start(), calls=%async_computation.11 | async-start | bytes 6488064 | tf_op jit(solution)/shard_map/all_gather | solution.py:53
  13.7 36.5 %copy-start.3 = (s32[1024]{0:T(1024)}, s32[1024]{0:T(1024)S(1)}, u32[]{:S(2)}) copy-start(s32[1024]{0:T(1024)S(1)} %pad_clamp_fusion) | copy-start | bytes 12292
  13.7 14.8 %copy-start.8 = (bf16[64,16,64]{2,1,0:T(8,128)(2,1)S(1)}, bf16[64,16,64]{2,1,0:T(8,128)(2,1)}, u32[]{:S(2)}) copy-start(bf16[64,16,64]{2,1,0:T(8,128)(2,1)} %param.37) | copy-start | bytes 393220
  15.7 16.9 %all-to-all-start.2 = ((bf16[32,2,512]{2,1,0:T(2,128)(2,1)}), bf16[32,2,512]{2,1,0:T(2,128)(2,1)S(1)}, u32[]{:S(2)}, u32[]{:S(2)}) async-start(bf16[32,2,512]{2,1,0:T(2,128)(2,1)} %reshape.344), calls=%async_computation.2 | async-start | bytes 131072 | tf_op jit(solution)/shard_map/all_to_all | solution.py:174
  25.3 160.4 %all-gather.11.cloned.1.call-start = ((), (), s32[]{:S(2)}) async-start(), calls=%async_computation.12 | async-start | bytes 2162688 | tf_op jit(solution)/shard_map/all_gather | solution.py:53
  32.6 13.7 %all-to-all-start = ((bf16[32,2,1536]{2,1,0:T(2,128)(2,1)}), bf16[32,2,1536]{2,1,0:T(2,128)(2,1)S(1)}, u32[]{:S(2)}, u32[]{:S(2)}) async-start(bf16[32,2,1536]{2,1,0:T(2,128)(2,1)} %reshape.338), calls=%async_computation | async-start | bytes 393216 | tf_op jit(solution)/shard_map/all_to_all | solution.py:173
  46.3 12.7 %all-to-all-start.3 = ((bf16[32,2,2048]{2,1,0:T(2,128)(2,1)}), bf16[32,2,2048]{2,1,0:T(2,128)(2,1)S(1)}, u32[]{:S(2)}, u32[]{:S(2)}) async-start(bf16[32,2,2048]{2,1,0:T(2,128)(2,1)} %reshape.342), calls=%async_computation.3 | async-start | bytes 524288 | tf_op jit(solution)/shard_map/all_to_all | solution.py:170
  59.0 18.1 %all-to-all-start.1 = ((bf16[32,2,6144]{2,1,0:T(2,128)(2,1)}), bf16[32,2,6144]{2,1,0:T(2,128)(2,1)S(1)}, u32[]{:S(2)}, u32[]{:S(2)}) async-start(bf16[32,2,6144]{2,1,0:T(2,128)(2,1)} %reshape.340), calls=%async_computation.1 | async-start | bytes 1572864 | tf_op jit(solution)/shard_map/all_to_all | solution.py:169
  62.7 175.6 %reduce-scatter.3.cloned.1.call-start = ((), (), s32[]{:S(2)}) async-start(), calls=%async_computation.13 | async-start | bytes 5242880 | tf_op jit(solution)/shard_map/reduce_scatter | solution.py:63
  62.8 20.2 %copy-start.20 = (f32[1024,4]{0,1:T(4,128)}, f32[1024,4]{0,1:T(4,128)S(1)}, u32[]{:S(2)}) copy-start(f32[1024,4]{0,1:T(4,128)S(1)} %get-tuple-element.429) | copy-start | bytes 49156
  62.8 63.8 %copy-start.16 = (bf16[1024,4]{0,1:T(4,128)(2,1)}, bf16[1024,4]{0,1:T(4,128)(2,1)S(1)}, u32[]{:S(2)}) copy-start(bf16[1024,4]{0,1:T(4,128)(2,1)S(1)} %get-tuple-element.428) | copy-start | bytes 24580
  86.8 39.8 %copy-start.25 = (f32[3,512]{1,0:T(4,128)S(1)}, f32[3,512]{1,0:T(4,128)}, u32[]{:S(2)}) copy-start(f32[3,512]{1,0:T(4,128)} %param.28) | copy-start | bytes 18436
  131.5 52.5 %copy-start.19 = (bf16[4,16,512]{2,1,0:T(8,128)(2,1)S(1)}, bf16[4,16,512]{2,1,0:T(8,128)(2,1)}, u32[]{:S(2)}) copy-start(bf16[4,16,512]{2,1,0:T(8,128)(2,1)} %squeeze.24) | copy-start | bytes 196612
  131.5 52.5 %copy-start.21 = (f32[1024,4]{0,1:T(4,128)S(1)}, f32[1024,4]{0,1:T(4,128)}, u32[]{:S(2)}) copy-start(f32[1024,4]{0,1:T(4,128)} %copy-done.20) | copy-start | bytes 49156
  193.0 45.3 %copy-start.2 = (bf16[256,2048]{1,0:T(8,128)(2,1)S(1)}, bf16[256,2048]{1,0:T(8,128)(2,1)}, u32[]{:S(2)}) copy-start(bf16[256,2048]{1,0:T(8,128)(2,1)} %param.24) | copy-start | bytes 3145732
  193.1 47.4 %copy-start.22 = (f32[2048]{0:T(1024)S(1)}, f32[2048]{0:T(1024)}, u32[]{:S(2)}) copy-start(f32[2048]{0:T(1024)} %param.31) | copy-start | bytes 24580
  193.1 47.4 %copy-start.23 = (f32[2048]{0:T(1024)S(1)}, f32[2048]{0:T(1024)}, u32[]{:S(2)}) copy-start(f32[2048]{0:T(1024)} %param.30) | copy-start | bytes 24580
  193.1 113.1 %all-gather.13.cloned.1.call-start = ((), (), s32[]{:S(2)}) async-start(), calls=%async_computation.14 | async-start | bytes 5242880 | tf_op jit(solution)/shard_map/all_gather | solution.py:59
  241.9 100.2 %all-gather.15.cloned.1.call-start = ((), (), s32[]{:S(2)}) async-start(), calls=%async_computation.15 | async-start | bytes 6488064 | tf_op jit(solution)/shard_map/all_gather | solution.py:53
  242.5 148.8 %all-gather.17.cloned.1.call-start = ((), (), s32[]{:S(2)}) async-start(), calls=%async_computation.16 | async-start | bytes 5947392 | tf_op jit(solution)/shard_map/all_gather | solution.py:53
  246.4 19.2 %copy-start.9 = (bf16[64,16,64]{2,1,0:T(8,128)(2,1)S(1)}, bf16[64,16,64]{2,1,0:T(8,128)(2,1)}, u32[]{:S(2)}) copy-start(bf16[64,16,64]{2,1,0:T(8,128)(2,1)} %param.41) | copy-start | bytes 393220
  246.4 15.3 %all-to-all-start.6 = ((bf16[32,2,704]{2,1,0:T(2,128)(2,1)}), bf16[32,2,704]{2,1,0:T(2,128)(2,1)S(1)}, u32[]{:S(2)}, u32[]{:S(2)}) async-start(bf16[32,2,704]{2,1,0:T(2,128)(2,1)} %reshape.352), calls=%async_computation.7 | async-start | bytes 196608 | tf_op jit(solution)/shard_map/all_to_all | solution.py:176
  255.4 22.3 %copy-start.5 = (bf16[64,32,64]{2,1,0:T(8,128)(2,1)S(1)}, bf16[64,32,64]{2,1,0:T(8,128)(2,1)}, u32[]{:S(2)}) copy-start(bf16[64,32,64]{2,1,0:T(8,128)(2,1)} %param.38) | copy-start | bytes 786436
  261.7 12.1 %all-to-all-start.4 = ((bf16[32,2,1408]{2,1,0:T(2,128)(2,1)}), bf16[32,2,1408]{2,1,0:T(2,128)(2,1)S(1)}, u32[]{:S(2)}, u32[]{:S(2)}) async-start(bf16[32,2,1408]{2,1,0:T(2,128)(2,1)} %reshape.346), calls=%async_computation.5 | async-start | bytes 360448 | tf_op jit(solution)/shard_map/all_to_all | solution.py:175
  273.8 12.7 %all-to-all-start.7 = ((bf16[32,2,2048]{2,1,0:T(2,128)(2,1)}), bf16[32,2,2048]{2,1,0:T(2,128)(2,1)S(1)}, u32[]{:S(2)}, u32[]{:S(2)}) async-start(bf16[32,2,2048]{2,1,0:T(2,128)(2,1)} %reshape.350), calls=%async_computation.8 | async-start | bytes 524288 | tf_op jit(solution)/shard_map/all_to_all | solution.py:172
  286.6 15.2 %all-to-all-start.5 = ((bf16[32,2,4096]{2,1,0:T(2,128)(2,1)}), bf16[32,2,4096]{2,1,0:T(2,128)(2,1)S(1)}, u32[]{:S(2)}, u32[]{:S(2)}) async-start(bf16[32,2,4096]{2,1,0:T(2,128)(2,1)} %reshape.348), calls=%async_computation.6 | async-start | bytes 1048576 | tf_op jit(solution)/shard_map/all_to_all | solution.py:171
  290.4 155.8 %reduce-scatter.5.cloned.1.call-start = ((), (), s32[]{:S(2)}) async-start(), calls=%async_computation.17 | async-start | bytes 5242880 | tf_op jit(solution)/shard_map/reduce_scatter | solution.py:63
  354.0 43.5 %copy-start.11 = (bf16[4,16,2048]{2,1,0:T(8,128)(2,1)S(1)}, bf16[4,16,2048]{2,1,0:T(8,128)(2,1)}, u32[]{:S(2)}) copy-start(bf16[4,16,2048]{2,1,0:T(8,128)(2,1)} %squeeze.28) | copy-start | bytes 786436
  400.7 48.1 %copy-start.1 = (bf16[64,48,64]{2,1,0:T(8,128)(2,1)S(1)}, bf16[64,48,64]{2,1,0:T(8,128)(2,1)}, u32[]{:S(2)}) copy-start(bf16[64,48,64]{2,1,0:T(8,128)(2,1)} %param.34) | copy-start | bytes 1179652
  (11 other events, 56.1 us)
Sparse Core Ops, SparseCore 0:
  12.6 51.2 all-gather.6
  66.1 50.0 all-gather.8
  118.5 42.3 all-gather.10
  193.2 45.1 reduce-scatter.2
  242.1 47.7 all-gather.12
  292.0 50.0 all-gather.14
  344.4 46.9 all-gather.16
  400.8 45.2 reduce-scatter.4
where the time goes:
time: 464 us; the launch traced here: 456 us
  waiting for transfers between devices  232 us (50%)
  matrix products  94.2 us (20%)
  local copies, waits for them, and re-layouts  54.4 us (12%)
  starting transfers between devices  42.7 us (9%)
  other arithmetic  18.1 us (4%)
  between operations  14.5 us (3%)
    all_gather x4, waiting for transfers between devices, contract_rows(): lax.all_gather(weight, 'req', axis=1, tiled=True)  99 us
    reduce_scatter x2, waiting for transfers between devices, reduce_rows(): lax.psum_scatter(partial_value.astype(jnp.bfloat16), 'tok', scatter_dimen...  90.7 us
    dot_general x4, matrix products, contract_rows(): jnp.einsum('tn,knc->tkc', operand, lax.all_gather(weight, 'req', axis=1,...  30 us
    dot_general x4, matrix products, key_block(): jnp.einsum('qhd,khd->hqk', query_part, key_part, preferred_element_type=j...  25.8 us
    dot_general x4, matrix products, key_block(): jnp.einsum('hqk,khd->qhd', weights.astype(jnp.bfloat16), value_part, pref...  20.4 us
    unnamed x75, local copies, waits for them, and re-layouts  19.4 us
    all_to_all x1, starting transfers between devices, on_device(): lax.all_to_all(picked[5], 'req', split_axis=0, concat_axis=3, tiled=True)  9.59 us
    dot_general x4, matrix products, low_rank(): jnp.einsum('tn,jkn->tjk', operand, shrink, preferred_element_type=jnp.flo...  9.45 us
  transfers between devices with their start and end apart: 16, of which 13 were waited for; matrix products, arithmetic and copies ran while one was open for 30% of the time, Pallas kernels for 0%

commit v1 on v0

v1 whole, which is shorter than its diff:
```python
import functools
import math

import jax
import jax.numpy as jnp
from jax import lax
from jax.experimental import pallas as pl
from jax.experimental.pallas import tpu as pltpu
from jax.sharding import PartitionSpec as P

HD = 64
ROT = 16
MESH = pl.DeviceIdType.MESH
VMEM = pl.BlockSpec(memory_space=pltpu.VMEM)
ANY = pl.BlockSpec(memory_space=pl.ANY)
SMEM = pl.BlockSpec(memory_space=pltpu.SMEM)
F32 = jnp.float32
BF16 = jnp.bfloat16


def layer_norm(values, gain_vec, shift_bias):
    row_mean = jnp.mean(values, axis=-1, keepdims=True)
    centered = values - row_mean
    variance = jnp.mean(centered * centered, axis=-1, keepdims=True)
    return centered * lax.rsqrt(variance + 1e-05) * gain_vec + shift_bias


def dot(left, right):
    return lax.dot_general(left, right, (((1,), (0,)), ((), ())), preferred_element_type=F32)


def dot_t(left, right):
    return lax.dot_general(left, right, (((1,), (1,)), ((), ())), preferred_element_type=F32)


def pick_kernel(ids, aq, wd, ag, wo, bq, bo, cg, cd, a_out, b_out, c_out):
    def eye(n):
        return (
            lax.broadcasted_iota(jnp.int32, (n, n), 0)
            == lax.broadcasted_iota(jnp.int32, (n, n), 1)
        ).astype(BF16)

    eye_a, eye_b, eye_c = eye(aq.shape[2]), eye(bq.shape[2]), eye(cg.shape[2])
    slots = 4

    def owner(g, carry):
        def rows(ref):
            return [ref[ids[g * slots + j]] for j in range(slots)]

        stack_a = jnp.concatenate(rows(aq) + rows(wd) + rows(ag) + rows(wo), axis=0)
        stack_b = jnp.concatenate(rows(bq) + rows(bo), axis=0)
        stack_c = jnp.concatenate(rows(cg) + rows(cd), axis=0)
        a_out[g] = dot_t(eye_a, stack_a).astype(BF16)
        b_out[g] = dot_t(eye_b, stack_b).astype(BF16)
        c_out[g] = dot_t(eye_c, stack_c).astype(BF16)
        return carry

    lax.fori_loop(0, a_out.shape[0], owner, 0)


def pick_adapters(ids, aq, wd, ag, wo, bq, bo, cg, cd):
    owners = ids.shape[0] // 4
    cols_a = 4 * (aq.shape[1] + wd.shape[1] + ag.shape[1] + wo.shape[1])
    cols_b = 4 * (bq.shape[1] + bo.shape[1])
    cols_c = 4 * (cg.shape[1] + cd.shape[1])
    return pl.pallas_call(
        pick_kernel,
        out_shape=[
            jax.ShapeDtypeStruct((owners, aq.shape[2], cols_a), BF16),
            jax.ShapeDtypeStruct((owners, bq.shape[2], cols_b), BF16),
            jax.ShapeDtypeStruct((owners, cg.shape[2], cols_c), BF16),
        ],
        in_specs=[SMEM] + [VMEM] * 8,
        out_specs=[VMEM] * 3,
        name="pick",
    )(ids, aq, wd, ag, wo, bq, bo, cg, cd)


def ring():
    n = lax.axis_size("tok")
    me = lax.axis_index("tok")
    return me, lax.rem(me + 1, n), lax.rem(me + n - 1, n), lax.rem(me + 2, n)


def greet(right, left):
    barrier = pltpu.get_barrier_semaphore()
    for neighbour in (left, right):
        pl.semaphore_signal(barrier, inc=1, device_id={"tok": neighbour}, device_id_type=MESH)
    pl.semaphore_wait(barrier, 2)


def send_to(source, target, send_sem, recv_sem, device):
    return pltpu.make_async_remote_copy(
        src_ref=source,
        dst_ref=target,
        send_sem=send_sem,
        recv_sem=recv_sem,
        device_id={"tok": device},
        device_id_type=MESH,
    )


def rows_of(block, rows, offset=0, size=None):
    return pl.ds(pl.multiple_of(block * rows + offset, rows // 2), rows if size is None else size)


class RingGather:
    def __init__(self, own, held, send, recv):
        me, right, left, opposite = ring()
        rows = own.shape[0]
        half = rows // 2
        low, high = pl.ds(0, half), pl.ds(half, half)
        mine_low = held.at[rows_of(me, rows, 0, half)]
        mine_high = held.at[rows_of(me, rows, half, half)]
        left_low = held.at[rows_of(left, rows, 0, half)]
        right_high = held.at[rows_of(right, rows, half, half)]
        self.first = [
            send_to(own.at[low], mine_low, send.at[0], recv.at[0], right),
            send_to(own.at[high], mine_high, send.at[1], recv.at[1], left),
            send_to(own.at[high], mine_high, send.at[2], recv.at[2], right),
            send_to(own.at[low], mine_low, send.at[3], recv.at[3], left),
        ]
        self.second = [
            send_to(left_low, left_low, send.at[4], recv.at[4], right),
            send_to(right_high, right_high, send.at[5], recv.at[5], left),
        ]

    def start(self):
        for copy in self.first:
            copy.start()

    def forward(self):
        for copy, onward in zip(self.first[:2], self.second):
            copy.wait_recv()
            onward.start()

    def neighbours(self):
        for copy in self.first[2:]:
            copy.wait_recv()

    def opposite(self):
        for copy in self.second:
            copy.wait_recv()

    def drain(self):
        for copy in self.first + self.second:
            copy.wait_send()


def gather_kernel(own, held, send, recv):
    me, right, left, _ = ring()
    greet(right, left)
    moves = RingGather(own, held, send, recv)
    moves.start()
    held[rows_of(me, own.shape[0]), :] = own[...]
    moves.forward()
    moves.neighbours()
    moves.opposite()
    moves.drain()


def gather_rows(own, count):
    rows, width = own.shape
    return pl.pallas_call(
        gather_kernel,
        out_shape=jax.ShapeDtypeStruct((rows * count, width), own.dtype),
        in_specs=[VMEM],
        out_specs=VMEM,
        scratch_shapes=[pltpu.SemaphoreType.DMA((6,)), pltpu.SemaphoreType.DMA((6,))],
        compiler_params=pltpu.CompilerParams(collective_id=0, has_side_effects=True),
        name="gather_rows",
    )(own)


def scatter_sum(term, total, far, to_right, to_left, mid_low, mid_high, from_left, from_right, send, recv):
    me, right, left, opposite = ring()
    rows = far.shape[0]
    half = rows // 2
    low, high = pl.ds(0, half), pl.ds(half, half)
    copies = [
        send_to(far.at[low], mid_low, send.at[0], recv.at[0], right),
        send_to(far.at[high], mid_high, send.at[1], recv.at[1], left),
        send_to(to_right.at[high], from_left.at[high], send.at[2], recv.at[2], right),
        send_to(to_left.at[low], from_right.at[low], send.at[3], recv.at[3], left),
        send_to(to_right.at[low], from_left.at[low], send.at[4], recv.at[4], right),
        send_to(to_left.at[high], from_right.at[high], send.at[5], recv.at[5], left),
    ]
    term(opposite, far)
    copies[0].start()
    copies[1].start()
    term(right, to_right)
    copies[2].start()
    term(left, to_left)
    copies[3].start()
    copies[0].wait_recv()
    to_right[low, :] = (to_right[low, :].astype(F32) + mid_low[...].astype(F32)).astype(BF16)
    copies[4].start()
    copies[1].wait_recv()
    to_left[high, :] = (to_left[high, :].astype(F32) + mid_high[...].astype(F32)).astype(BF16)
    copies[5].start()
    term(me, total)
    for copy in copies[2:]:
        copy.wait_recv()
    for copy in copies:
        copy.wait_send()
    total[...] = total[...] + from_left[...].astype(F32) + from_right[...].astype(F32)


def sum_scratch(rows, width):
    half = rows // 2
    return [
        pltpu.VMEM((rows, width), F32),
        pltpu.VMEM((rows, width), BF16),
        pltpu.VMEM((rows, width), BF16),
        pltpu.VMEM((rows, width), BF16),
        pltpu.VMEM((half, width), BF16),
        pltpu.VMEM((half, width), BF16),
        pltpu.VMEM((rows, width), BF16),
        pltpu.VMEM((rows, width), BF16),
        pltpu.SemaphoreType.DMA((6,)),
        pltpu.SemaphoreType.DMA((6,)),
    ]


def of_slot(slot, columns, per_slot):
    owner = lax.broadcasted_iota(jnp.int32, (slot.shape[0], columns), 1) // per_slot
    return slot == owner


def attention_kernel(
    x_ref, w_ref, bias_ref, narrow_ref, widen_ref, cos_ref, up_ref, down_ref, slot_ref, keyslot_ref,
    out_ref, q_s, k_s, v_s, bias_s,
):
    step = pl.program_id(0)
    rows = x_ref.shape[0]
    width = out_ref.shape[1]
    pairs = width // 128
    x = x_ref[...]
    slot = slot_ref[pl.ds(pl.multiple_of(step * rows, rows), rows), :]
    columns = narrow_ref.shape[1]
    low = dot(x, narrow_ref[...])
    low = jnp.where(of_slot(slot, columns, columns // 4), low, 0.0)
    kind = (lax.broadcasted_iota(jnp.int32, low.shape, 1) // 16) % 3
    here = pl.ds(pl.multiple_of(step * rows, rows), rows)
    cosine, rise, fall = cos_ref[...], up_ref[...], down_ref[...]
    lane = lax.broadcasted_iota(jnp.int32, (rows, 128), 1)
    for i in range(3):
        part = dot(x, w_ref[:, i * width : (i + 1) * width]) + bias_ref[i : i + 1, :]
        part = part + dot_t(jnp.where(kind == i, low, 0.0).astype(BF16), widen_ref[...])
        for p in range(pairs):
            block = part[:, p * 128 : (p + 1) * 128]
            if i < 2:
                block = (
                    block * cosine
                    + pltpu.roll(block, 120, 1) * rise
                    + pltpu.roll(block, 8, 1) * fall
                )
            block = block.astype(BF16)
            if i == 0:
                zero = jnp.zeros_like(block)
                q_s[2 * p] = jnp.where(lane < 64, block, zero)
                q_s[2 * p + 1] = jnp.where(lane < 64, zero, block)
            elif i == 1:
                k_s[p, here, :] = block
            else:
                v_s[p, here, 0:128] = block
                v_s[p, here, 128:256] = jnp.ones_like(block)

    scale = HD ** (-0.5) * math.log2(math.e)

    def window(start, count):
        keys = pl.ds(pl.multiple_of(start * rows, rows), count * rows)
        span = (rows, count * rows)
        query_place = lax.broadcasted_iota(jnp.int32, span, 0) + step * rows
        key_place = lax.broadcasted_iota(jnp.int32, span, 1) + start * rows
        visible = (slot == keyslot_ref[:, keys]) & (key_place <= query_place)
        bias_s[:, : count * rows] = jnp.where(visible, 0.0, -jnp.inf)

        def pair(p, carry):
            key = k_s[p, keys, :]
            value = v_s[p, keys, :]
            both = []
            for side in range(2):
                scores = dot_t(q_s[2 * p + side], key)
                weight = jnp.exp2(scores * scale + bias_s[:, : count * rows]).astype(BF16)
                both.append(dot(weight, value))
            even = both[0][:, :128] / both[0][:, 128:]
            odd = both[1][:, :128] / both[1][:, 128:]
            out_ref[:, pl.ds(pl.multiple_of(p * 128, 128), 128)] = jnp.where(
                lane < 64, even, odd
            ).astype(BF16)
            return carry

        lax.fori_loop(0, pairs, pair, 0)

    @pl.when(step == 0)
    def _():
        window(0, 1)

    @pl.when(step == 1)
    def _():
        window(0, 2)

    @pl.when(step >= 2)
    def _():
        window(step - 2, 3)


def attend(x, first, width, bias, narrow, widen, cosine, rise, fall, slot, keyslot):
    count, depth = x.shape
    rows = 256
    pairs = width // 128
    table = pl.BlockSpec((rows, 128), lambda i: (i, 0))
    whole = lambda a: pl.BlockSpec(a.shape, lambda i: (0, 0))
    return pl.pallas_call(
        attention_kernel,
        out_shape=jax.ShapeDtypeStruct((count, width), BF16),
        grid=(count // rows,),
        in_specs=[
            pl.BlockSpec((rows, depth), lambda i: (i, 0)),
            pl.BlockSpec((depth, 3 * width), lambda i: (0, 0)),
            whole(bias),
            whole(narrow),
            whole(widen),
            table,
            table,
            table,
            whole(slot),
            whole(keyslot),
        ],
        out_specs=pl.BlockSpec((rows, width), lambda i: (i, 0)),
        scratch_shapes=[
            pltpu.VMEM((2 * pairs, rows, 128), BF16),
            pltpu.VMEM((pairs, count, 128), BF16),
            pltpu.VMEM((pairs, count, 256), BF16),
            pltpu.VMEM((rows, 3 * rows), F32),
        ],
        compiler_params=pltpu.CompilerParams(dimension_semantics=("arbitrary",)),
        name="attend",
    )(x, first, bias, narrow, widen, cosine, rise, fall, slot, keyslot)


def output_kernel(
    att, first, narrow, widen, slot, tokens, gain, shift, residual, normed,
    weight, low_s, weight_sem, *scratch,
):
    me, right, left, _ = ring()
    shares = first.shape[0]
    width = first.shape[3]
    load = pltpu.make_async_copy(first.at[:, :, :, :], weight, weight_sem)
    load.start()
    greet(right, left)
    low = dot(att[...], narrow[...])
    columns = low.shape[1]
    low_s[...] = jnp.where(of_slot(slot[...], columns, columns // 4), low, 0.0).astype(BF16)
    load.wait()
    rows = tokens.shape[0]
    blocks = tokens.shape[1] // width

    def term(block, ref):
        here = rows_of(block, rows)

        def column(q, carry):
            at = pl.ds(pl.multiple_of(q * width, width), width)
            matrix = weight[:, q].reshape(att.shape[1], width)
            value = dot(att[here, :], matrix) + dot_t(low_s[here, :], widen[at, :])
            ref[:, at] = value.astype(ref.dtype)
            return carry

        lax.fori_loop(0, blocks, column, 0)

    total = scratch[0]
    scatter_sum(term, *scratch)
    for part in range(4):
        here = pl.ds(part * rows // 4, rows // 4)
        kept = (tokens[here, :].astype(F32) + total[here, :]).astype(BF16)
        residual[here, :] = kept
        normed[here, :] = layer_norm(kept.astype(F32), gain[...], shift[...]).astype(BF16)


def project(att, first, narrow, widen, slot, tokens, gain, shift):
    rows, width = tokens.shape
    shape = jax.ShapeDtypeStruct((rows, width), BF16)
    return pl.pallas_call(
        output_kernel,
        out_shape=[shape, shape],
        in_specs=[VMEM, ANY] + [VMEM] * 6,
        out_specs=[VMEM, VMEM],
        scratch_shapes=[
            pltpu.VMEM(first.shape, BF16),
            pltpu.VMEM((att.shape[0], narrow.shape[1]), BF16),
            pltpu.SemaphoreType.DMA,
        ]
        + sum_scratch(rows, width),
        compiler_params=pltpu.CompilerParams(collective_id=1, has_side_effects=True),
        name="project",
    )(att, first, narrow, widen, slot, tokens, gain, shift)


def feed_kernel(
    own, residual, second, down, narrow_gate, widen_gate, narrow_down, widen_down, slot, out,
    weight, held, hidden, low_s, weight_sem, gather_send, gather_recv, *scratch,
):
    me, right, left, opposite = ring()
    load = pltpu.make_async_copy(second.at[:, pl.ds(0, weight.shape[1])], weight, weight_sem)
    load.start()
    greet(right, left)
    moves = RingGather(own, held, gather_send, gather_recv)
    moves.start()
    rows, width = own.shape
    units = hidden.shape[1]
    held[rows_of(me, rows), :] = own[...]
    load.wait()

    def widen(block):
        here = rows_of(block, rows)
        x = held[here, :]
        low = dot(x, narrow_gate[...])
        columns = low.shape[1]
        low = jnp.where(of_slot(slot[here, :], columns, columns // 4), low, 0.0)
        kind = (lax.broadcasted_iota(jnp.int32, low.shape, 1) // 16) % 2
        both = dot(x, weight[...])
        gate = both[:, :units] + dot_t(jnp.where(kind == 0, low, 0.0).astype(BF16), widen_gate[...])
        up = both[:, units:] + dot_t(jnp.where(kind == 1, low, 0.0).astype(BF16), widen_gate[...])
        value = (gate / (1.0 + jnp.exp(-gate)) * up).astype(BF16)
        hidden[here, :] = value
        low_down = dot(value, narrow_down[...])
        columns = low_down.shape[1]
        low_s[here, :] = jnp.where(
            of_slot(slot[here, :], columns, columns // 4), low_down, 0.0
        ).astype(BF16)

    widen(me)
    moves.forward()
    moves.neighbours()

    def near(i, carry):
        widen(lax.rem(me + 1 + 2 * i, 4))
        return carry

    lax.fori_loop(0, 2, near, 0)
    moves.opposite()
    widen(opposite)
    moves.drain()
    step = 512

    def term(block, ref):
        here = rows_of(block, rows)

        def column(q, carry):
            at = pl.ds(pl.multiple_of(q * step, step), step)
            value = dot(hidden[here, :], down[:, at]) + dot_t(low_s[here, :], widen_down[at, :])
            ref[:, at] = value.astype(ref.dtype)
            return carry

        lax.fori_loop(0, width // step, column, 0)

    scatter_sum(term, *scratch)
    out[...] = (residual[...].astype(F32) + scratch[0][...]).astype(BF16)


def feed(own, residual, second, down, narrow_gate, widen_gate, narrow_down, widen_down, slot):
    rows, width = own.shape
    count = slot.shape[0]
    units = down.shape[0]
    return pl.pallas_call(
        feed_kernel,
        out_shape=jax.ShapeDtypeStruct((rows, width), BF16),
        in_specs=[VMEM, VMEM, ANY] + [VMEM] * 6,
        out_specs=VMEM,
        scratch_shapes=[
            pltpu.VMEM((second.shape[0], 2 * units), BF16),
            pltpu.VMEM((count, width), BF16),
            pltpu.VMEM((count, units), BF16),
            pltpu.VMEM((count, narrow_down.shape[1]), BF16),
            pltpu.SemaphoreType.DMA,
            pltpu.SemaphoreType.DMA((6,)),
            pltpu.SemaphoreType.DMA((6,)),
        ]
        + sum_scratch(rows, width),
        compiler_params=pltpu.CompilerParams(collective_id=2, has_side_effects=True),
        name="feed",
    )(own, residual, second, down, narrow_gate, widen_gate, narrow_down, widen_down, slot)


def rotation_tables(positions):
    half = ROT // 2
    frequency = jnp.exp(-math.log(10000.0) * (2.0 * jnp.arange(half, dtype=F32) / ROT))
    angles = positions.astype(F32)[:, None] * frequency[None, :]
    cosine, sine = jnp.cos(angles), jnp.sin(angles)
    count = positions.shape[0]
    zero = jnp.zeros((count, half), F32)
    rest = jnp.zeros((count, HD - ROT), F32)
    cos_head = jnp.concatenate([cosine, cosine, rest + 1.0], axis=1)
    rise_head = jnp.concatenate([-sine, zero, rest], axis=1)
    fall_head = jnp.concatenate([zero, sine, rest], axis=1)
    return [jnp.concatenate([t, t], axis=1) for t in (cos_head, rise_head, fall_head)]


def on_device(
    tokens,
    attention_norm_gain,
    attention_norm_bias,
    query_key_value_matrix,
    query_key_value_bias,
    output_matrix,
    feedforward_norm_gain,
    feedforward_norm_bias,
    gate_up_matrix,
    down_matrix,
    adapter_input_query_key_value,
    adapter_output_query_key_value,
    adapter_input_output,
    adapter_output_projection,
    adapter_input_gate_up,
    adapter_output_gate_up,
    adapter_input_down,
    adapter_output_down,
    lengths,
    adapter_per_request,
):
    tok_count = lax.axis_size("tok")
    owners = lax.axis_size("req")
    rows, width = tokens.shape
    count = rows * tok_count
    share = query_key_value_matrix.shape[1]
    head_cols = query_key_value_matrix.shape[2]
    units = gate_up_matrix.shape[2]
    fold = width // head_cols
    qkv = jnp.transpose(query_key_value_matrix, (1, 0, 2)).reshape(share, 3 * head_cols)
    out_rows = output_matrix.shape[1]
    out_fold = jnp.transpose(
        output_matrix[0].reshape(out_rows, fold, head_cols), (1, 0, 2)
    ).reshape(share, head_cols)
    first = lax.all_gather(
        jnp.concatenate([qkv, out_fold], axis=1), "req", axis=0, tiled=True
    )
    gate_up = jnp.transpose(gate_up_matrix, (1, 0, 2)).reshape(share, 2 * units)
    down_rows = down_matrix.shape[1]
    down_pad = jnp.pad(down_matrix[0], ((0, share // 2 - down_rows), (0, 0)))
    down_fold = jnp.concatenate([down_pad[:, : width // 2], down_pad[:, width // 2 :]], axis=0)
    second_part = jnp.concatenate([gate_up, down_fold], axis=1)
    second_part, first = lax.optimization_barrier((second_part, first))
    second = lax.all_gather(second_part, "req", axis=0, tiled=True)

    def flat(divided):
        return divided.reshape(divided.shape[0], divided.shape[1], divided.shape[3])

    ids = adapter_per_request.reshape(-1)
    pack_a, pack_b, pack_c = pick_adapters(
        ids,
        adapter_input_query_key_value,
        adapter_output_down,
        adapter_input_gate_up,
        adapter_output_projection,
        flat(adapter_output_query_key_value),
        flat(adapter_input_output),
        flat(adapter_output_gate_up),
        flat(adapter_input_down),
    )

    def trade(pack):
        return lax.all_to_all(pack, "req", split_axis=0, concat_axis=0, tiled=True).reshape(
            owners * pack.shape[1], pack.shape[2]
        )

    got_a, got_b, got_c = trade(pack_a), trade(pack_b), trade(pack_c)
    c_qkv = 4 * adapter_input_query_key_value.shape[1]
    c_one = 4 * adapter_output_down.shape[1]
    c_two = 4 * adapter_input_gate_up.shape[1]
    narrow_qkv = got_a[:, :c_qkv]
    widen_down = got_a[:, c_qkv : c_qkv + c_one]
    narrow_gate = got_a[:, c_qkv + c_one : c_qkv + c_one + c_two]
    widen_out = got_a[:, c_qkv + c_one + c_two :]
    widen_qkv, narrow_out = got_b[:, :c_qkv], got_b[:, c_qkv:]
    widen_gate, narrow_down = got_c[:, :c_two], got_c[:, c_two:]

    request_end = jnp.cumsum(lengths[0])
    request_begin = request_end - lengths[0]
    places = jnp.arange(count, dtype=jnp.int32)
    slot = jnp.sum((places[:, None] >= request_end[None, :]).astype(jnp.int32), axis=1)
    member = slot[:, None] == jnp.arange(lengths.shape[1], dtype=jnp.int32)[None, :]
    begin = jnp.sum(jnp.where(member, request_begin[None, :], 0), axis=1)
    cosine, rise, fall = rotation_tables(places - begin)
    slot_column, slot_row = slot[:, None], slot[None, :]

    normed = layer_norm(tokens.astype(F32), attention_norm_gain, attention_norm_bias).astype(BF16)
    gathered = gather_rows(normed, tok_count)
    attended = attend(
        gathered, first, head_cols, query_key_value_bias, narrow_qkv, widen_qkv,
        cosine, rise, fall, slot_column, slot_row,
    )
    out_shares = first[:, 3 * head_cols :].reshape(owners, fold, out_rows, head_cols)
    residual, normed2 = project(
        attended, out_shares, narrow_out, widen_out, slot_column, tokens,
        feedforward_norm_gain[None], feedforward_norm_bias[None],
    )
    down = (
        second[:, 2 * units :]
        .reshape(owners, 2, share // 2, width // 2)[:, :, :down_rows, :]
        .transpose(0, 2, 1, 3)
        .reshape(owners * down_rows, width)
    )
    return feed(
        normed2, residual, second, down, narrow_gate, widen_gate, narrow_down, widen_down, slot_column
    )


def solution(mesh):
    in_specs = (
        P(("req", "tok"), None),
        P(),
        P(),
        P(None, "req", "tok"),
        P(None, "tok"),
        P("tok", "req", None),
        P(),
        P(),
        P(None, "req", "tok"),
        P("tok", "req", None),
        P(None, None, "req"),
        P(None, None, "tok", "req"),
        P(None, None, "tok", "req"),
        P(None, None, "req"),
        P(None, None, "req"),
        P(None, None, "tok", "req"),
        P(None, None, "tok", "req"),
        P(None, None, "req"),
        P("req", None),
        P(),
    )
    out_specs = P(("req", "tok"), None)
    return jax.shard_map(
        on_device, mesh=mesh, in_specs=in_specs, out_specs=out_specs, check_vma=False
    )
```

time: 464 us -> 349 us (0.75); the launches traced: 456 us -> 346 us
  Pallas kernels: 0 us -> 195 us
  waiting for transfers between devices: 232 us -> 77.1 us
  matrix products: 94.2 us -> 0 us
  starting transfers between devices: 42.7 us -> 15.1 us
  local copies, waits for them, and re-layouts: 54.4 us -> 38.5 us
  other arithmetic: 18.1 us -> 5.81 us
    pallas_call x0 -> x5, Pallas kernels: none -> 195 us  [the longest x1 77.5 us: feed(): pl.pallas_call(feed_kernel, out_shape=jax.ShapeDtypeStruct((rows, width),...]
    dot_general x20 -> x0, matrix products: 94.2 us -> none  [the longest x4 30 us: contract_rows(): jnp.einsum('tn,knc->tkc', operand, lax.all_gather(weight, 'req', axis=1,...]
    reduce_scatter x2 -> x0, waiting for transfers between devices: 90.7 us -> none  [reduce_rows(): lax.psum_scatter(partial_value.astype(jnp.bfloat16), 'tok', scatter_dimen...]
    all_gather x6 -> x2, waiting for transfers between devices: 99.1 us -> 54.8 us  [the longest x1 54.8 us: on_device(): lax.all_gather(jnp.concatenate([qkv, out_fold], axis=1), 'req', axis=0, t...]
    all_to_all x8 -> x3, starting transfers between devices: 42 us -> 15.1 us  [trade(): lax.all_to_all(pack, 'req', split_axis=0, concat_axis=0, tiled=True)]
    all_to_all x8 -> x3, waiting for transfers between devices: 40 us -> 22.3 us  [trade(): lax.all_to_all(pack, 'req', split_axis=0, concat_axis=0, tiled=True)]
    slice x4 -> x11, local copies, waits for them, and re-layouts: 0.96 us -> 14.4 us  [the longest x1 3.04 us: on_device(): first[:, 3 * head_cols:].reshape(owners, fold, out_rows, head_cols)]
    all_to_all x10 -> x0, local copies, waits for them, and re-layouts: 9.49 us -> none  [the longest x2 2.59 us: on_device(): lax.all_to_all(picked[4], 'req', split_axis=0, concat_axis=3, tiled=True)]
  transfers between devices with their start and end apart: 16 -> 5, of which waited for: 13 -> 3; matrix products, arithmetic and copies ran while one was open for 30% -> 9% of each run, Pallas kernels for 0% -> 34%
where the time goes in v1:
time: 349 us; the launch traced here: 346 us
  Pallas kernels  195 us (56%)
  waiting for transfers between devices  77.1 us (22%)
  local copies, waits for them, and re-layouts  38.5 us (11%)
  starting transfers between devices  15.1 us (4%)
  between operations  13.7 us (4%)
  other arithmetic  5.81 us (2%)
    pallas_call x1, Pallas kernels, feed(): pl.pallas_call(feed_kernel, out_shape=jax.ShapeDtypeStruct((rows, width),...  77.5 us
    all_gather x1, waiting for transfers between devices, on_device(): lax.all_gather(jnp.concatenate([qkv, out_fold], axis=1), 'req', axis=0, t...  54.8 us
    pallas_call x1, Pallas kernels, project(): pl.pallas_call(output_kernel, out_shape=[shape, shape], in_specs=[VMEM, A...  43.3 us
    pallas_call x1, Pallas kernels, gather_rows(): pl.pallas_call(gather_kernel, out_shape=jax.ShapeDtypeStruct((rows * coun...  40.3 us
    pallas_call x1, Pallas kernels, attend(): pl.pallas_call(attention_kernel, out_shape=jax.ShapeDtypeStruct((count, w...  23.6 us
    all_to_all x3, waiting for transfers between devices, trade(): lax.all_to_all(pack, 'req', split_axis=0, concat_axis=0, tiled=True)  22.3 us
    all_to_all x3, starting transfers between devices, trade(): lax.all_to_all(pack, 'req', split_axis=0, concat_axis=0, tiled=True)  15.1 us
    unnamed x36, local copies, waits for them, and re-layouts  13.8 us
  transfers between devices with their start and end apart: 5, of which 3 were waited for; matrix products, arithmetic and copies ran while one was open for 9% of the time, Pallas kernels for 34%

profile of v1, /device:TPU:1, one launch (start us, length us, event | category | flops | bytes accessed | tf_op | source)
XLA Modules:
  0.0 345.7 jit_solution(12309623318009264605)
XLA Ops:
  6.5 1.0 copy.68
  7.5 0.9 reshape_squeeze.3
  9.3 1.1 copy.54
  11.4 54.8 %all-gather.3.cloned.1.call-done.w_ref = bf16[2048,2048]{1,0:T(8,128)(2,1)} async-done(((bf16[64,2048]{1,0:T(8,128)(2,1)}), bf16[2048,2048]{1,0:T(8,128)(2,1)}) %all-gather.3.cloned.1.call-update) | async-done | bytes 8388624 | tf_op jit(solution)/shard_map/all_gather | solution.py:535
  66.2 1.4 copy.58
  67.6 1.7 copy.60
  69.3 0.9 copy.59
  70.2 1.0 copy.61
  71.9 10.8 %pick.1 = (bf16[32,64,448]{2,1,0:T(8,128)(2,1)}, bf16[32,16,256]{2,1,0:T(8,128)(2,1)}, bf16[32,22,192]{2,1,0:T(8,128)(2,1)}) custom-call(s32[128]{0:T(128)} %reshape.82.ids, bf16[64,48,64]{2,1,0:T(8,128)(2,1)} %aq.1, bf16[64,16,64]{2,1,0:T(8,128)(2,1)} %wd.1, bf16[64,32,64]{2,1,0:T(8,128)(2,1)} %ag.1, bf16[64,16,64]{2,1,0:T(8,128)(2,1)} %wo.1, ...), custom_call_target="tpu_custom_call" | custom-call | tf_op jit(solution)/shard_map/pick/pallas_call | solution.py:66
  82.7 5.5 %all-to-all-start.1 = ((bf16[32,16,256]{2,1,0:T(8,128)(2,1)}), bf16[32,16,256]{2,1,0:T(8,128)(2,1)S(1)}, u32[]{:S(2)}, u32[]{:S(2)}) async-start(bf16[32,16,256]{2,1,0:T(8,128)(2,1)} %get-tuple-element.14), calls=%async_computation.1 | async-start | bytes 524288 | tf_op jit(solution)/shard_map/all_to_all | solution.py:563
  88.4 8.7 %all-to-all-done.1 = bf16[32,16,256]{2,1,0:T(8,128)(2,1)S(1)} async-done(((bf16[32,16,256]{2,1,0:T(8,128)(2,1)}), bf16[32,16,256]{2,1,0:T(8,128)(2,1)S(1)}, u32[]{:S(2)}, u32[]{:S(2)}) %all-to-all-start.1) | async-done | bytes 262176 | tf_op jit(solution)/shard_map/all_to_all | solution.py:563
  97.1 3.8 %all-to-all-start.2 = ((bf16[32,22,192]{2,1,0:T(8,128)(2,1)}), bf16[32,22,192]{2,1,0:T(8,128)(2,1)S(1)}, u32[]{:S(2)}, u32[]{:S(2)}) async-start(bf16[32,22,192]{2,1,0:T(8,128)(2,1)} %get-tuple-element.18), calls=%async_computation.2 | async-start | bytes 786432 | tf_op jit(solution)/shard_map/all_to_all | solution.py:563
  101.1 13.6 %all-to-all-done.2 = bf16[32,22,192]{2,1,0:T(8,128)(2,1)S(1)} async-done(((bf16[32,22,192]{2,1,0:T(8,128)(2,1)}), bf16[32,22,192]{2,1,0:T(8,128)(2,1)S(1)}, u32[]{:S(2)}, u32[]{:S(2)}) %all-to-all-start.2) | async-done | bytes 270368 | tf_op jit(solution)/shard_map/all_to_all | solution.py:563
  115.4 5.8 %all-to-all-start = ((bf16[32,64,448]{2,1,0:T(8,128)(2,1)}), bf16[32,64,448]{2,1,0:T(8,128)(2,1)}, u32[]{:S(2)}, u32[]{:S(2)}) async-start(bf16[32,64,448]{2,1,0:T(8,128)(2,1)} %get-tuple-element.13), calls=%async_computation | async-start | bytes 4194304 | tf_op jit(solution)/shard_map/all_to_all | solution.py:563
  121.2 1.9 multiply_sine_fusion
  123.2 1.7 concatenate.28.up_ref
  125.0 1.7 concatenate.29.down_ref
  126.7 1.0 copy.63.slot_ref.slot
  128.5 1.4 fusion.5.own
  129.9 40.3 %gather_rows.1.x_ref = bf16[1024,2048]{1,0:T(8,128)(2,1)} custom-call(bf16[256,2048]{1,0:T(8,128)(2,1)} %fusion.5.own), custom_call_target="tpu_custom_call" | custom-call | tf_op jit(solution)/shard_map/gather_rows/pallas_call | solution.py:164
  170.2 1.8 concatenate.27.cos_ref
  174.3 2.3 slice.52.narrow_ref
  176.6 1.9 slice.58.narrow_gate
  178.4 2.4 fusion.8
  180.8 3.0 slice.43
  183.9 23.6 %attend.1.att = bf16[1024,512]{1,0:T(8,128)(2,1)} custom-call(bf16[1024,2048]{1,0:T(8,128)(2,1)} %gather_rows.1.x_ref, bf16[2048,2048]{1,0:T(8,128)(2,1)} %all-gather.3.cloned.1.call-done.w_ref, f32[3,512]{1,0:T(4,128)} %bias_ref.1, bf16[2048,192]{1,0:T(8,128)(2,1)} %slice.52.narrow_ref, bf16[512,192]{1,0:T(8,128)(2,1)} %bitcast.40, ...), custom_call_target="tpu_custom_call" | custom-call | tf_op jit(solution)/shard_map/attend/pallas_call | solution.py:315
  207.5 43.3 %project.1 = (bf16[256,2048]{1,0:T(8,128)(2,1)}, bf16[256,2048]{1,0:T(8,128)(2,1)}) custom-call(bf16[1024,512]{1,0:T(8,128)(2,1)} %attend.1.att, bf16[32,4,16,512]{3,2,1,0:T(8,128)(2,1)} %bitcast.36, bf16[512,64]{1,0:T(8,128)(2,1)} %slice.54.narrow, bf16[2048,64]{1,0:T(8,128)(2,1)} %get-tuple-element.20.widen, s32[1024,1]{1,0:T(8,128)} %copy.63.slot_ref.slot, ...), custom_call_target="tpu_custom_call" | custom-call | tf_op jit(solution)/shard_map/project/pallas_call | solution.py:384
  250.9 2.2 slice-done
  253.6 3.0 copy.67
  256.6 2.5 copy.69
  259.1 77.5 %feed.1 = bf16[256,2048]{1,0:T(8,128)(2,1)} custom-call(bf16[256,2048]{1,0:T(8,128)(2,1)} %get-tuple-element.15.own, bf16[256,2048]{1,0:T(8,128)(2,1)} %get-tuple-element.16.residual, bf16[2048,2432]{1,0:T(8,128)(2,1)} %all-gather.5.cloned.1.call-done.second, bf16[704,2048]{1,0:T(8,128)(2,1)} %bitcast.35, bf16[2048,128]{1,0:T(8,128)(2,1)} %slice.58.narrow_gate, ...), custom_call_target="tpu_custom_call" | custom-call | tf_op jit(solution)/shard_map/feed/pallas_call | solution.py:466
  336.6 2.3 copy.71
  (60 shorter events, 7.2 us)
Async XLA Ops:
  6.5 4.1 %copy-start.6 = (bf16[1,22,2048]{2,1,0:T(8,128)(2,1)S(1)}, bf16[1,22,2048]{2,1,0:T(8,128)(2,1)}, u32[]{:S(2)}) copy-start(bf16[1,22,2048]{2,1,0:T(8,128)(2,1)} %param.29) | copy-start | bytes 270340
  6.5 59.6 %copy-start.4 = (bf16[64,48,1,16]{0,3,2,1:T(8,128)(2,1)S(1)}, bf16[64,48,1,16]{0,3,2,1:T(8,128)(2,1)}, u32[]{:S(2)}) copy-start(bf16[64,48,1,16]{0,3,2,1:T(8,128)(2,1)} %param.31) | copy-start | bytes 294916
  6.5 59.6 %all-gather.3.cloned.1.call-start = ((), (), s32[]{:S(2)}) async-start(), calls=%async_computation.3 | async-start | bytes 8650752 | tf_op jit(solution)/shard_map/all_gather | solution.py:535
  6.5 61.1 %copy-start.5 = (bf16[64,32,1,22]{0,1,3,2:T(8,128)(2,1)S(1)}, bf16[64,32,1,22]{0,1,3,2:T(8,128)(2,1)}, u32[]{:S(2)}) copy-start(bf16[64,32,1,22]{0,1,3,2:T(8,128)(2,1)} %param.35) | copy-start | bytes 270340
  8.4 60.8 %copy-start.9 = (bf16[64,16,1,16]{0,3,2,1:T(8,128)(2,1)S(1)}, bf16[64,16,1,16]{0,3,2,1:T(8,128)(2,1)}, u32[]{:S(2)}) copy-start(bf16[64,16,1,16]{0,3,2,1:T(8,128)(2,1)} %param.32) | copy-start | bytes 98308
  9.2 61.1 %copy-start.7 = (bf16[64,16,1,22]{0,1,3,2:T(8,128)(2,1)S(1)}, bf16[64,16,1,22]{0,1,3,2:T(8,128)(2,1)}, u32[]{:S(2)}) copy-start(bf16[64,16,1,22]{0,1,3,2:T(8,128)(2,1)} %param.36) | copy-start | bytes 135172
  9.2 241.6 %all-gather.5.cloned.1.call-start = ((), (), s32[]{:S(2)}) async-start(), calls=%async_computation.4 | async-start | bytes 10272768 | tf_op jit(solution)/shard_map/all_gather | solution.py:544
  9.3 62.0 %copy-start.12 = (s32[32,4]{0,1:T(4,128)S(1)}, s32[32,4]{0,1:T(4,128)}, u32[]{:S(2)}) copy-start(s32[32,4]{0,1:T(4,128)} %param.39) | copy-start | bytes 1540
  71.9 16.3 %copy-start.13 = (s32[1,4]{1,0:T(1,128)S(1)}, s32[1,4]{1,0:T(1,128)}, u32[]{:S(2)}) copy-start(s32[1,4]{1,0:T(1,128)} %param.38) | copy-start | bytes 52
  82.7 14.4 %all-to-all-start.1 = ((bf16[32,16,256]{2,1,0:T(8,128)(2,1)}), bf16[32,16,256]{2,1,0:T(8,128)(2,1)S(1)}, u32[]{:S(2)}, u32[]{:S(2)}) async-start(bf16[32,16,256]{2,1,0:T(8,128)(2,1)} %get-tuple-element.14), calls=%async_computation.1 | async-start | bytes 524288 | tf_op jit(solution)/shard_map/all_to_all | solution.py:563
  97.1 74.9 %copy-start.1 = (bf16[32,16,256]{2,1,0:T(8,128)(2,1)}, bf16[32,16,256]{2,1,0:T(8,128)(2,1)S(1)}, u32[]{:S(2)}) copy-start(bf16[32,16,256]{2,1,0:T(8,128)(2,1)S(1)} %all-to-all-done.1) | copy-start | bytes 786436
  97.1 17.6 %all-to-all-start.2 = ((bf16[32,22,192]{2,1,0:T(8,128)(2,1)}), bf16[32,22,192]{2,1,0:T(8,128)(2,1)S(1)}, u32[]{:S(2)}, u32[]{:S(2)}) async-start(bf16[32,22,192]{2,1,0:T(8,128)(2,1)} %get-tuple-element.18), calls=%async_computation.2 | async-start | bytes 786432 | tf_op jit(solution)/shard_map/all_to_all | solution.py:563
  101.0 25.8 %copy-start.8 = (s32[1024]{0:T(1024)}, s32[1024]{0:T(1024)S(1)}, u32[]{:S(2)}) copy-start(s32[1024]{0:T(1024)S(1)} %convert_reduce_fusion.1) | copy-start | bytes 12292
  114.7 0.8 copy-start.2
  115.4 58.9 %all-to-all-start = ((bf16[32,64,448]{2,1,0:T(8,128)(2,1)}), bf16[32,64,448]{2,1,0:T(8,128)(2,1)}, u32[]{:S(2)}, u32[]{:S(2)}) async-start(bf16[32,64,448]{2,1,0:T(8,128)(2,1)} %get-tuple-element.13), calls=%async_computation | async-start | bytes 4194304 | tf_op jit(solution)/shard_map/all_to_all | solution.py:563
  125.0 2.8 copy-start
  126.7 1.7 copy-start.10
  126.7 1.7 copy-start.11
  170.2 2.5 copy-start.3
  250.9 2.2 slice-start
Sparse Core Ops, SparseCore 0:
  9.6 56.4 all-gather.2
  68.4 69.9 all-gather.4
